TPU v7x, 32 devices: a whole 2x2x4 slice. The times are simulated.
32 devices in a mesh: rep: 4 (over x, core), shard: 8 (over z, y).
Axes of the slice: x: 2, y: 2, z: 4, core: 2. Of those that a mesh axis runs over, the one named last changes fastest.
Arguments:
- tokens: bfloat16 [32768, 768], P(('rep', 'shard')), may hold values from -6 to 6
- segment_ids: int32 [32, 1024], P(('rep', 'shard')), may hold values from 0 to 3, never falling along the last dimension, each value on 1 to 768 neighbouring positions
- norm1_gain: bfloat16 [768], P('shard'), may hold values from 0.5 to 1.5
- norm1_shift: bfloat16 [768], P('shard'), may hold values from -1.75 to 1.75
- w_qkv: bfloat16 [768, 2304], P('shard'), may hold values from -0.21875 to 0.21875
- q_bias: bfloat16 [768], P('shard'), may hold values from -3 to 3
- v_bias: bfloat16 [768], P('shard'), may hold values from -3 to 3
- w_out: bfloat16 [768, 768], P('shard'), may hold values from -0.875 to 0.875
- out_bias: bfloat16 [768], P('shard'), may hold values from -3 to 3
- norm2_gain: bfloat16 [768], P('shard'), may hold values from 0.5 to 1.5
- norm2_shift: bfloat16 [768], P('shard'), may hold values from -1.75 to 1.75
- w_fc: bfloat16 [768, 3072], P('shard'), may hold values from -0.21875 to 0.21875
- fc_bias: bfloat16 [3072], P('shard'), may hold values from -3 to 3
- w_proj: bfloat16 [3072, 768], P('shard'), may hold values from -0.109375 to 0.109375
- proj_bias: bfloat16 [768], P('shard'), may hold values from -3 to 3
- cotangent: bfloat16 [32768, 768], P(('rep', 'shard')), may hold values from -6 to 6
Outputs:
- layer_out: bfloat16 [32768, 768], P(('rep', 'shard'))
- grad_tokens: bfloat16 [32768, 768], P(('rep', 'shard'))
- grad_norm1_gain: float32 [768], P('shard')
- grad_norm1_shift: float32 [768], P('shard')
- grad_w_qkv: float32 [768, 2304], P('shard')
- grad_q_bias: float32 [768], P('shard')
- grad_v_bias: float32 [768], P('shard')
- grad_w_out: float32 [768, 768], P('shard')
- grad_out_bias: float32 [768], P('shard')
- grad_norm2_gain: float32 [768], P('shard')
- grad_norm2_shift: float32 [768], P('shard')
- grad_w_fc: float32 [768, 3072], P('shard')
- grad_fc_bias: float32 [3072], P('shard')
- grad_w_proj: float32 [3072, 768], P('shard')
- grad_proj_bias: float32 [768], P('shard')
All inputs are finite; a program needn't handle non-finite values.
Results may differ from a plain program's by a relative error of at most 0.014.
Values may be sent and summed in bfloat16 or wider, within the bound.
A program may use at most 320 MiB of HBM per device.

v0:
```python
from functools import partial

import jax
import jax.numpy as jnp
from jax import lax
from jax.experimental import pallas as pl
from jax.experimental.pallas import tpu as pltpu
from jax.sharding import PartitionSpec as P

HEAD = 64
EPSILON = 1e-05
QUERY_BLOCK = 256
ROW_CHUNK = 256
MASKED = -1e30
GELU_SCALE = 0.7978845608028654
GELU_CUBE = 0.044715
VMEM_LIMIT = 62 << 20
NN = (((1,), (0,)), ((), ()))
NT = (((1,), (1,)), ((), ()))
f32 = jnp.float32
bf16 = jnp.bfloat16
WHOLE = pl.BlockSpec(memory_space=pltpu.VMEM)

GAIN1, SHIFT1, BIAS_Q, BIAS_V, BIAS_OUT, GAIN2, SHIFT2, BIAS_PROJ, BIAS_FC = range(9)


def matmul(left, right, dims):
    return lax.dot_general(left, right, dims, preferred_element_type=f32)


def normalized(values):
    centred = values - jnp.mean(values, axis=-1, keepdims=True)
    inverse = lax.rsqrt(jnp.mean(centred * centred, axis=-1, keepdims=True) + EPSILON)
    return centred * inverse, inverse


def norm_pull(grad_normed, gain_row, norm, inverse):
    scaled = grad_normed * gain_row
    return inverse * (
        scaled
        - jnp.mean(scaled, axis=-1, keepdims=True)
        - norm * jnp.mean(scaled * norm, axis=-1, keepdims=True)
    )


def chunk(number):
    return pl.ds(pl.multiple_of(number * ROW_CHUNK, ROW_CHUNK), ROW_CHUNK)


def total(values):
    return jnp.sum(values, axis=0, keepdims=True)


def block(index, size):
    return pl.ds(pl.multiple_of(index * size, size), size)


def build_mask(segment_ref, mask_ref):
    length = segment_ref.shape[1]
    query_seg = segment_ref[...].astype(f32)
    key_seg = jnp.transpose(jnp.broadcast_to(query_seg, (8, length)))[:, 0:1]
    for start in range(0, length, QUERY_BLOCK):
        stop = start + QUERY_BLOCK
        key_at = lax.broadcasted_iota(jnp.int32, (stop, QUERY_BLOCK), 0)
        query_at = lax.broadcasted_iota(jnp.int32, (stop, QUERY_BLOCK), 1) + start
        allowed = (key_seg[0:stop] == query_seg[:, start:stop]) & (key_at <= query_at)
        mask_ref[0:stop, start:stop] = jnp.where(allowed, 0.0, MASKED)


def half_lanes(which):
    lane = lax.broadcasted_iota(jnp.int32, (1, 2 * HEAD), 1)
    return (lane < HEAD) if which == 0 else (lane >= HEAD)


def keep_half(values, which):
    return jnp.where(half_lanes(which), values, jnp.zeros_like(values))


def attend_forward(
    pair, queries, keys, values_t_ref, mask_ref, attended_t_ref, lse_ref, tick=lambda number: None
):
    length = keys.shape[0]
    queries = queries * bf16(HEAD**-0.5)
    for which in range(2):
        tick(which)
        head_queries = keep_half(queries, which)
        rows = block(2 * pair + which, HEAD)
        values_t = values_t_ref[rows, :]
        for start in range(0, length, QUERY_BLOCK):
            stop = start + QUERY_BLOCK
            scores = matmul(keys[0:stop], head_queries[start:stop], NT)
            scores = scores + mask_ref[0:stop, start:stop]
            top = jnp.max(scores, axis=0, keepdims=True)
            terms = jnp.exp(scores - top)
            sums = jnp.sum(terms, axis=0, keepdims=True)
            mixed = matmul(values_t[:, 0:stop], terms.astype(bf16), NN)
            attended_t_ref[rows, start:stop] = (mixed * (1.0 / sums)).astype(bf16)
            lse_ref[pl.ds(2 * pair + which, 1), start:stop] = top + jnp.log(sums)


def attend_backward(
    pair,
    operands,
    keys_t_ref,
    mask_ref,
    lse_ref,
    dots_ref,
    grad_queries_t_ref,
    grad_keys_ref,
    grad_values_ref,
    tick=lambda number: None,
):
    queries, keys, values, grads = operands
    length, scale_by = keys.shape[0], HEAD**-0.5
    queries = queries * bf16(scale_by)
    for number, start in enumerate(reversed(range(0, length, QUERY_BLOCK))):
        tick(number)
        stop = start + QUERY_BLOCK
        grad_keys = grad_values = 0.0
        for which in range(2):
            head = pl.ds(2 * pair + which, 1)
            rows = block(2 * pair + which, HEAD)
            query_rows = keep_half(queries[start:stop], which)
            grad_rows = keep_half(grads[start:stop], which)
            scores = matmul(keys[0:stop], query_rows, NT)
            probs = jnp.exp(scores + mask_ref[0:stop, start:stop] - lse_ref[head, start:stop])
            grad_probs = matmul(values[0:stop], grad_rows, NT)
            grad_scores = (probs * (grad_probs - dots_ref[head, start:stop])).astype(bf16)
            grad_values = grad_values + matmul(probs.astype(bf16), grad_rows, NN)
            grad_keys = grad_keys + matmul(grad_scores, query_rows, NN)
            grad_queries_t_ref[rows, start:stop] = (
                matmul(keys_t_ref[rows, 0:stop], grad_scores, NN) * scale_by
            ).astype(bf16)
        if stop == length:
            grad_keys_ref[...] = grad_keys
            grad_values_ref[...] = grad_values
        else:
            grad_keys_ref[0:stop] += grad_keys
            grad_values_ref[0:stop] += grad_values


MESH = pl.DeviceIdType.MESH
HBM = pl.BlockSpec(memory_space=pl.ANY)


def flip(value, bits):
    bit = 1
    while bit <= bits:
        if bits & bit:
            value = value + bit - 2 * bit * ((value // bit) % 2)
        bit *= 2
    return value


class Place:
    def __init__(self, shards):
        self.lines = shards // 2
        self.rep, self.me = lax.axis_index("rep"), lax.axis_index("shard")
        self.far, self.core = self.rep // 2, self.rep % 2
        self.line, self.side = self.me // 2, self.me % 2

    def shard(self, hop, turn):
        return flip(self.line, hop) * 2 + flip(self.side, turn)

    def peer(self, hop, turn):
        return (self.rep, self.shard(hop, turn))

    def across(self):
        return ((1 - self.far) * 2 + self.core, self.me)

    def sibling(self):
        return (self.far * 2 + 1 - self.core, self.me)

    def others(self):
        return [(h, t) for h in range(self.lines) for t in range(2) if h or t]

    def meet(self, peers):
        barrier = pltpu.get_barrier_semaphore()
        for peer in peers:
            pl.semaphore_signal(barrier, inc=1, device_id=peer, device_id_type=MESH)
        pl.semaphore_wait(barrier, len(peers))


def aligned(start, size):
    return pl.ds(pl.multiple_of(start, 16), size)


def remote(src, dst, send, recv, peer):
    return pltpu.make_async_remote_copy(
        src_ref=src,
        dst_ref=dst,
        send_sem=send,
        recv_sem=recv,
        device_id=peer,
        device_id_type=MESH,
    )


def cut(count):
    half = count // 2
    return half // 3 // 16 * 16, half


class Gather:
    def __init__(self, place, own, full, send, recv, local):
        self.place, self.own, self.full = place, own, full
        self.send, self.recv, self.local = send, recv, local
        self.hops = range(1, place.lines)

    def rows(self, at, kind, far, core):
        edge, half = cut(self.own[at].shape[0])
        if kind == "wide":
            return aligned(core * half + far * edge, half - edge)
        if kind == "edge":
            return aligned(core * half + far * (half - edge), edge)
        return aligned(core * half, half)

    def copy(self, at, stage, hop, turn, arriving=False):
        place, lines = self.place, self.place.lines
        number = hop * 2 + turn
        far, core = place.far, place.core
        if stage == "line":
            slot, peer, kind = hop - 1, place.peer(hop, 0), "wide"
            shard = place.shard(hop if arriving else 0, 0)
        elif stage == "side":
            slot, peer, kind = lines - 1 + hop, place.peer(0, 1), "wide"
            shard = place.shard(hop, 1 if arriving else 0)
        elif stage == "far":
            slot, peer, kind = 2 * lines - 1 + number - 1, place.across(), "edge"
            shard = place.shard(hop, turn)
            far = 1 - far if arriving else far
        else:
            slot, peer, kind = 4 * lines - 2 + number - 1, place.sibling(), "half"
            shard = place.shard(hop, turn)
            core = 1 - core if arriving else core
        rows = self.rows(at, kind, far, core)
        target = self.full[at].at[shard, rows]
        mine = not arriving and (stage == "line" or (stage == "side" and hop == 0))
        source = self.own[at].at[rows] if mine else target
        return remote(source, target, self.send.at[at, slot], self.recv.at[at, slot], peer)

    def start(self, at, stage, hop, turn=0):
        self.copy(at, stage, hop, turn).start()

    def got(self, at, stage, hop, turn=0):
        self.copy(at, stage, hop, turn, arriving=True).wait_recv()

    def keep(self, at):
        return pltpu.make_async_copy(
            self.own[at], self.full[at].at[self.place.me], self.local.at[at]
        )

    def own_side(self, at):
        self.start(at, "side", 0)

    def first(self, at, hop):
        self.start(at, "line", hop)

    def line(self, at, hop):
        self.got(at, "line", hop)
        self.start(at, "side", hop)
        self.start(at, "far", hop, 0)

    def side(self, at, hop):
        self.got(at, "side", hop)
        self.start(at, "far", hop, 1)

    def far(self, at, hop, turn):
        self.got(at, "far", hop, turn)
        self.start(at, "core", hop, turn)

    def last(self, at):
        for hop, turn in self.place.others():
            self.got(at, "core", hop, turn)
        self.keep(at).wait()

    def drain(self, at):
        for hop in self.hops:
            self.copy(at, "line", hop, 0).wait_send()
        for hop in range(self.place.lines):
            self.copy(at, "side", hop, 0).wait_send()
        for hop, turn in self.place.others():
            self.copy(at, "far", hop, turn).wait_send()
            self.copy(at, "core", hop, turn).wait_send()


def add_into(into, other):
    into[...] = (into[...].astype(f32) + other[...].astype(f32)).astype(bf16)


class Summed:
    def __init__(self, place, grad, done, buffers, send, recv, source=None, load_sem=None):
        self.place, self.grad, self.done = place, grad, done
        self.send_sem, self.recv_sem = send, recv
        self.source = grad if source is None else source
        self.load_sem = load_sem
        (
            self.from_core,
            self.from_far,
            self.from_side,
            self.from_me,
            self.from_line,
            self.from_back,
        ) = buffers
        self.edge_size, self.half = cut(grad.shape[1])
        self.hops = range(1, place.lines)

    def rows(self, kind, far=None, core=None):
        far = self.place.far if far is None else far
        core = self.place.core if core is None else core
        edge, half = self.edge_size, self.half
        if kind == "wide":
            return aligned(core * half + far * edge, half - edge)
        if kind == "edge":
            return aligned(core * half + far * (half - edge), edge)
        return aligned(core * half, half)

    def pair_of(self, hop):
        return pl.ds(2 * flip(self.place.line, hop), 2)

    def copy(self, stage, hop=0):
        place, lines, grad = self.place, self.place.lines, self.grad
        if stage == "core":
            slot, peer = 0, place.sibling()
            pair = self.source.at[:, self.rows("half", core=1 - place.core)], self.from_core
        elif stage == "far":
            slot, peer = hop, place.across()
            pair = (
                grad.at[self.pair_of(hop), self.rows("edge", far=1 - place.far)],
                self.from_far.at[hop - 1],
            )
        elif stage == "side":
            slot, peer = lines + hop, place.peer(0, 1)
            source = grad.at[place.shard(hop, 1), self.rows("wide" if hop else "half")]
            pair = source, self.from_side.at[hop - 1] if hop else self.from_me
        elif stage == "line":
            slot, peer = 2 * lines + hop - 1, place.peer(hop, 0)
            pair = grad.at[place.shard(hop, 0), self.rows("wide")], self.from_line.at[hop - 1]
        elif stage == "back":
            slot, peer = 3 * lines - 1, place.across()
            pair = grad.at[place.me, self.rows("half")], self.from_back
        else:
            slot, peer = 3 * lines, place.sibling()
            mine = self.done.at[self.rows("half")]
            pair = mine, mine
        return remote(*pair, self.send_sem.at[slot], self.recv_sem.at[slot], peer)

    def load(self):
        rows = self.rows("half")
        return pltpu.make_async_copy(
            self.source.at[:, rows], self.grad.at[:, rows], self.load_sem
        )

    def begin(self):
        self.copy("core").start()
        if self.load_sem is not None:
            self.load().start()

    def core(self):
        self.copy("core").wait_recv()
        if self.load_sem is not None:
            self.load().wait()
        for shard in range(2 * self.place.lines):
            add_into(self.grad.at[shard, self.rows("half")], self.from_core.at[shard])

    def me0(self):
        self.copy("side", 0).start()

    def send(self, hop):
        self.copy("far", hop).start()

    def far(self, hop):
        self.copy("far", hop).wait_recv()
        add_into(self.grad.at[self.pair_of(hop), self.rows("edge")], self.from_far.at[hop - 1])
        self.copy("side", hop).start()

    def side(self, hop):
        self.copy("side", hop).wait_recv()
        mine = self.grad.at[self.place.shard(hop, 0), self.rows("wide")]
        add_into(mine, self.from_side.at[hop - 1])
        self.copy("line", hop).start()

    def me(self):
        self.copy("side", 0).wait_recv()
        add_into(self.grad.at[self.place.me, self.rows("half")], self.from_me)

    def lines(self):
        mine = self.grad.at[self.place.me, self.rows("wide")]
        sums = mine[...].astype(f32)
        for hop in self.hops:
            self.copy("line", hop).wait_recv()
            sums = sums + self.from_line[hop - 1].astype(f32)
        mine[...] = sums.astype(bf16)
        self.copy("back").start()

    def back(self):
        self.copy("back").wait_recv()
        mine = self.grad[self.place.me, self.rows("half")].astype(f32)
        self.done[self.rows("half")] = (mine + self.from_back[...].astype(f32)).astype(bf16)
        self.copy("pair").start()

    def finish(self):
        other = self.done.at[self.rows("half", core=1 - self.place.core)]
        slot = 3 * self.place.lines
        remote(
            other, other, self.send_sem.at[slot], self.recv_sem.at[slot], self.place.sibling()
        ).wait_recv()

    def drain(self):
        self.copy("core").wait_send()
        for hop in self.hops:
            self.copy("far", hop).wait_send()
            self.copy("line", hop).wait_send()
        for hop in range(self.place.lines):
            self.copy("side", hop).wait_send()
        self.copy("back").wait_send()
        self.copy("pair").wait_send()


SUM_BUFFERS = 6


def sum_buffers(lines, shards, rows, columns):
    edge, half = cut(rows)
    return [
        pltpu.VMEM((shards, half, columns), bf16),
        pltpu.VMEM((lines - 1, 2, edge, columns), bf16),
        pltpu.VMEM((lines - 1, half - edge, columns), bf16),
        pltpu.VMEM((half, columns), bf16),
        pltpu.VMEM((lines - 1, half - edge, columns), bf16),
        pltpu.VMEM((half, columns), bf16),
    ]


def sum_sems(lines, items):
    return [pltpu.SemaphoreType.DMA((items, 3 * lines + 1))] * 2


def first_norm(tokens_ref, params_ref, normed_ref):
    length, width = tokens_ref.shape
    row = lambda at: params_ref[at : at + 1, 0:width]

    @pl.loop(0, length // ROW_CHUNK)
    def _(number):
        norm, _ = normalized(tokens_ref[chunk(number)].astype(f32))
        normed_ref[chunk(number)] = (norm * row(GAIN1) + row(SHIFT1)).astype(bf16)


def forward_kernel(
    tokens_ref,
    segment_ref,
    params_ref,
    w_qkv_ref,
    projected_ref,
    attended_t_ref,
    lse_ref,
    mask_ref,
    normed_ref,
    values_t_ref,
):
    length, width = tokens_ref.shape
    pairs = width // (2 * HEAD)
    row = lambda at: params_ref[at : at + 1, 0:width]
    first_norm(tokens_ref, params_ref, normed_ref)
    for part, bias in enumerate((row(BIAS_Q), 0.0, row(BIAS_V))):
        columns = slice(part * width, (part + 1) * width)
        projected_ref[:, columns] = (
            matmul(normed_ref[...], w_qkv_ref[:, columns], NN) + bias
        ).astype(bf16)
    values_t_ref[...] = jnp.transpose(projected_ref[:, 2 * width :])
    build_mask(segment_ref, mask_ref)

    @pl.loop(0, pairs)
    def _(pair):
        attend_forward(
            pair,
            projected_ref[:, block(pair, 2 * HEAD)],
            projected_ref[:, block(pairs + pair, 2 * HEAD)],
            values_t_ref,
            mask_ref,
            attended_t_ref,
            lse_ref,
        )


GROUP = 4 * HEAD
GATHERED_EARLY = 1
SUMMED_EARLY = 1


(
    OWN,
    FIRST,
    LINE,
    SIDE,
    FAR,
    LAST,
    BEGIN_SUM,
    CORE_SUM,
    ME0_SUM,
    SEND_SUM,
    FAR_SUM,
    SIDE_SUM,
    ME_SUM,
    LINES_SUM,
    BACK_SUM,
    FINISH_SUM,
) = range(16)
P0, P1, P2, H0, H1, H2, H3, E0, E1, E2, E3, B0, B1, B2, B3, NEED, END = range(100, 117)

FORWARD_PLAN = {P0: [(OWN, 0), (FIRST, 0, 1)],
 P1: [(FIRST, 0, 3), (OWN, 1)],
 P2: [(FIRST, 0, 2), (LINE, 0, 1), (SIDE, 0, 0)],
 END: [(LAST, 5)],
 NEED: {0: [(FIRST, 1, 1), (SIDE, 1, 0), (OWN, 2), (OWN, 3), (FIRST, 1, 3), (LINE, 0, 3), (FIRST, 1, 2),
            (FAR, 0, 1, 0), (FAR, 0, 0, 1), (FAR, 1, 0, 1), (OWN, 4), (SIDE, 0, 1), (FAR, 0, 3, 0),
            (FIRST, 2, 1), (LINE, 1, 1), (SIDE, 2, 0), (SIDE, 3, 0), (LINE, 0, 2), (FAR, 0, 1, 1),
            (FIRST, 2, 3), (SIDE, 0, 3), (FIRST, 2, 2), (OWN, 5), (FAR, 1, 1, 0), (FAR, 2, 0, 1),
            (LINE, 1, 3), (SIDE, 4, 0), (FIRST, 3, 1), (FAR, 3, 0, 1), (FAR, 0, 2, 0), (SIDE, 1, 1),
            (FAR, 0, 3, 1), (LINE, 1, 2), (FIRST, 3, 3), (SIDE, 0, 2), (LINE, 2, 1), (FIRST, 3, 2),
            (FAR, 1, 3, 0), (FAR, 4, 0, 1), (SIDE, 5, 0), (FAR, 1, 1, 1), (SIDE, 1, 3), (LINE, 2, 3),
            (FAR, 1, 2, 0), (FIRST, 4, 1), (LINE, 2, 2), (FAR, 0, 2, 1), (FAR, 2, 1, 0), (SIDE, 1, 2),
            (LINE, 3, 1), (SIDE, 2, 1), (FIRST, 4, 3), (FAR, 5, 0, 1), (LAST, 0)]},
 0: {0: [(FIRST, 4, 2)],
     1: [(LAST, 1), (LINE, 4, 1), (FIRST, 5, 3)],
     2: [(FAR, 2, 2, 1), (FAR, 2, 3, 1), (SIDE, 3, 2), (SIDE, 3, 3), (FAR, 3, 2, 0), (FAR, 3, 3, 0),
         (FAR, 3, 1, 1), (LINE, 4, 2), (SIDE, 4, 1), (FAR, 4, 1, 0), (FAR, 4, 3, 0)],
     3: [(SIDE, 4, 2), (LINE, 5, 2), (FAR, 3, 2, 1)],
     4: [(LAST, 3), (FAR, 4, 2, 1), (SIDE, 5, 2), (FAR, 5, 2, 0), (FAR, 5, 3, 0), (FAR, 5, 1, 1)],
     5: [(LAST, 4), (FAR, 5, 2, 1)]},
 1: {0: [(FAR, 1, 2, 1), (FAR, 1, 3, 1), (SIDE, 2, 2), (SIDE, 2, 3), (FAR, 2, 2, 0), (FAR, 2, 3, 0),
         (FAR, 2, 1, 1), (LINE, 3, 2), (SIDE, 3, 1), (FAR, 3, 1, 0), (LINE, 3, 3), (FIRST, 5, 1)],
     1: [(LINE, 4, 3), (FIRST, 5, 2)],
     2: [(SIDE, 4, 3), (LAST, 2), (LINE, 5, 1)],
     3: [(FAR, 3, 3, 1), (FAR, 4, 2, 0), (FAR, 4, 1, 1), (FAR, 4, 3, 1), (LINE, 5, 3), (FAR, 5, 1, 0),
         (SIDE, 5, 1)],
     4: [(SIDE, 5, 3)],
     5: [(FAR, 5, 3, 1)]}}

HIDDEN_PLAN = {H0: [(OWN, 0), (FIRST, 0, 1), (FIRST, 0, 3)],
 H1: [(FIRST, 0, 2), (OWN, 1)],
 H2: [(LINE, 0, 1), (SIDE, 0, 0), (FIRST, 1, 1)],
 H3: [(FIRST, 1, 3), (OWN, 2)],
 E0: [(FINISH_SUM, 0)],
 E3: [(BACK_SUM, 1)],
 END: [(FINISH_SUM, 1)],
 1: {0: [(LINE, 0, 3), (FAR, 0, 1, 0), (FIRST, 1, 2), (SIDE, 1, 0)],
     1: [(SIDE, 2, 2), (FAR, 2, 2, 0), (LINE, 3, 3), (SEND_SUM, 1, 3)]},
 2: {0: [(LINE, 0, 2), (SIDE, 0, 1), (FAR, 0, 0, 1)],
     1: [(LINE, 3, 2), (SIDE, 3, 1)],
     2: [(LINES_SUM, 0), (SIDE_SUM, 1, 2), (SIDE_SUM, 1, 1)]},
 3: {0: [(FAR, 0, 3, 0), (LINE, 1, 1), (FIRST, 2, 1), (SIDE, 2, 0)],
     1: [(FAR, 2, 2, 1), (FAR, 2, 3, 1), (FAR, 3, 1, 0), (FAR_SUM, 0, 2), (SIDE_SUM, 0, 3),
         (SEND_SUM, 1, 2)]},
 4: {0: [(SIDE, 0, 3), (FAR, 0, 2, 0), (FAR, 1, 0, 1), (FIRST, 2, 3), (OWN, 3)],
     1: [(SIDE, 3, 3), (FAR, 3, 3, 0), (FAR_SUM, 0, 1), (SEND_SUM, 1, 1)]},
 5: {0: [(SIDE, 0, 2), (FAR, 0, 1, 1), (FAR, 1, 1, 0), (FIRST, 2, 2), (BEGIN_SUM, 0)],
     1: [(LAST, 2), (SIDE, 3, 2), (FAR, 3, 2, 0), (FAR, 3, 1, 1), (ME0_SUM, 1)]},
 6: {0: [(LINE, 1, 3), (SIDE, 1, 1), (FAR, 2, 0, 1), (FIRST, 3, 1), (BEGIN_SUM, 1)],
     1: [(SIDE_SUM, 0, 2), (FAR_SUM, 1, 3)],
     2: [(BACK_SUM, 0)]},
 7: {0: [(FAR, 0, 3, 1), (LINE, 1, 2), (SIDE, 3, 0)],
     1: [(FAR, 3, 3, 1), (SIDE_SUM, 0, 1), (FAR_SUM, 1, 2)],
     2: [(LINES_SUM, 1)]},
 NEED: {1: [(FAR, 0, 2, 1), (FAR, 1, 3, 0), (FAR, 1, 1, 1), (LINE, 2, 1), (FIRST, 3, 3), (CORE_SUM, 0),
            (SEND_SUM, 0, 3), (CORE_SUM, 1), (SIDE, 1, 3), (FAR, 1, 2, 0), (ME0_SUM, 0), (LAST, 0),
            (FAR, 3, 0, 1), (SEND_SUM, 0, 2), (SIDE, 1, 2), (FAR, 2, 1, 0), (FIRST, 3, 2), (LINE, 2, 3),
            (SIDE, 2, 1), (FAR, 1, 3, 1), (LINE, 2, 2), (SEND_SUM, 0, 1), (ME_SUM, 0), (LINE, 3, 1),
            (FAR, 1, 2, 1), (SIDE, 2, 3), (FAR, 2, 3, 0), (FAR_SUM, 0, 3), (LAST, 1), (FAR, 2, 1, 1)],
        2: [(FAR, 3, 2, 1), (FAR_SUM, 1, 1), (ME_SUM, 1), (SIDE_SUM, 1, 3), (LAST, 3)]}}

BACKWARD_PLAN = {B0: [(BEGIN_SUM, 0), (BEGIN_SUM, 1), (BEGIN_SUM, 2), (BEGIN_SUM, 3), (BEGIN_SUM, 4)],
 B2: [(CORE_SUM, 0), (ME0_SUM, 0), (SEND_SUM, 0, 3), (SEND_SUM, 0, 2)],
 B3: [(SEND_SUM, 0, 1), (CORE_SUM, 1), (ME0_SUM, 1)],
 E0: [(SIDE_SUM, 4, 1), (FAR_SUM, 6, 3), (FAR_SUM, 6, 2), (BEGIN_SUM, 7)],
 E1: [(BACK_SUM, 2), (SIDE_SUM, 5, 3), (FAR_SUM, 6, 1)],
 E2: [(FINISH_SUM, 2), (LINES_SUM, 3), (SIDE_SUM, 5, 2), (ME_SUM, 6), (CORE_SUM, 7), (ME0_SUM, 7),
      (SEND_SUM, 7, 3)],
 E3: [(SIDE_SUM, 5, 1), (SEND_SUM, 7, 2)],
 END: [(SIDE_SUM, 6, 3), (SEND_SUM, 7, 1), (BACK_SUM, 3), (ME_SUM, 7), (LINES_SUM, 4), (SIDE_SUM, 6, 2),
       (FAR_SUM, 7, 3), (FINISH_SUM, 3), (FAR_SUM, 7, 2), (SIDE_SUM, 6, 1), (FAR_SUM, 7, 1), (SIDE_SUM, 7, 3),
       (BACK_SUM, 4), (SIDE_SUM, 7, 2), (LINES_SUM, 5), (FINISH_SUM, 4), (SIDE_SUM, 7, 1), (BACK_SUM, 5),
       (FINISH_SUM, 5), (LINES_SUM, 6), (LINES_SUM, 7), (BACK_SUM, 6), (FINISH_SUM, 6), (BACK_SUM, 7),
       (FINISH_SUM, 7)],
 1: {0: [(FAR_SUM, 0, 3), (SEND_SUM, 1, 3), (CORE_SUM, 2), (ME_SUM, 0), (SEND_SUM, 1, 2), (ME0_SUM, 2),
         (CORE_SUM, 3)],
     1: [(FAR_SUM, 0, 1), (FAR_SUM, 1, 3), (SEND_SUM, 2, 2)],
     2: [(SIDE_SUM, 1, 3), (SIDE_SUM, 1, 2), (FAR_SUM, 2, 2), (SEND_SUM, 3, 1), (SEND_SUM, 4, 3)],
     3: [(SIDE_SUM, 2, 3), (FAR_SUM, 3, 3), (SEND_SUM, 4, 1)],
     4: [(FINISH_SUM, 0), (LINES_SUM, 1), (SIDE_SUM, 3, 3), (FAR_SUM, 4, 3), (FAR_SUM, 4, 2)],
     5: [(BACK_SUM, 1), (SIDE_SUM, 3, 1), (FAR_SUM, 5, 3), (FAR_SUM, 5, 2)]},
 2: {0: [(SEND_SUM, 1, 1), (CORE_SUM, 4), (ME_SUM, 1), (FAR_SUM, 0, 2)],
     1: [(FAR_SUM, 1, 2), (SEND_SUM, 2, 1), (ME_SUM, 2)],
     2: [(FAR_SUM, 2, 1), (SEND_SUM, 4, 2), (CORE_SUM, 5), (SIDE_SUM, 1, 1)],
     3: [(FAR_SUM, 3, 2), (SEND_SUM, 5, 3)],
     4: [(FAR_SUM, 4, 1), (CORE_SUM, 6), (SEND_SUM, 6, 3), (SEND_SUM, 6, 2), (SIDE_SUM, 3, 2)],
     5: [(FINISH_SUM, 1), (LINES_SUM, 2), (SIDE_SUM, 4, 3), (FAR_SUM, 5, 1)]},
 3: {0: [(SEND_SUM, 2, 3)],
     1: [(SIDE_SUM, 0, 2), (SEND_SUM, 3, 3)],
     2: [(LINES_SUM, 0), (ME0_SUM, 3)],
     3: [(SIDE_SUM, 2, 2), (FAR_SUM, 3, 1), (SEND_SUM, 5, 2)],
     4: [(ME_SUM, 4), (ME0_SUM, 5), (SEND_SUM, 6, 1)],
     5: [(ME_SUM, 5), (SIDE_SUM, 4, 2), (ME0_SUM, 6)]},
 0: {1: [(SIDE_SUM, 0, 3)],
     2: [(SIDE_SUM, 0, 1), (FAR_SUM, 1, 1), (FAR_SUM, 2, 3), (SEND_SUM, 3, 2), (BEGIN_SUM, 5)],
     4: [(BACK_SUM, 0), (SIDE_SUM, 2, 1), (ME_SUM, 3), (ME0_SUM, 4), (SEND_SUM, 5, 1), (BEGIN_SUM, 6)]}}


class Runner:
    def __init__(self, plan, gather, sums):
        self.plan, self.gather, self.sums = plan, gather, sums

    def act(self, events):
        gather = self.gather
        for what, item, *where in events:
            if what >= BEGIN_SUM:
                one = self.sums[item]
                acts = (
                    one.begin,
                    one.core,
                    one.me0,
                    one.send,
                    one.far,
                    one.side,
                    one.me,
                    one.lines,
                    one.back,
                    one.finish,
                )
                acts[what - BEGIN_SUM](*where)
            else:
                acts = (
                    gather.own_side,
                    gather.first,
                    gather.line,
                    gather.side,
                    gather.far,
                    gather.last,
                )
                acts[what](item, *where)

    def do(self, key):
        self.act(self.plan.get(key, ()))

    def at_step(self, step, key):
        self.on(step, self.plan.get(key, {}))

    def on(self, step, table):
        for number, events in table.items():

            @pl.when(step == number)
            def _(events=events):
                self.act(events)


def gather_forward_kernel(
    shards,
    tokens_ref,
    segment_ref,
    own_params_ref,
    own_qkv_ref,
    own_out_ref,
    own_fc_ref,
    own_proj_ref,
    projected_ref,
    attended_t_ref,
    lse_ref,
    params_ref,
    full_qkv_ref,
    full_out_ref,
    full_fc_ref,
    full_proj_ref,
    mask_ref,
    normed_ref,
    values_t_ref,
    held_ref,
    weights_ref,
    tables_ref,
    group_ref,
    own_block_ref,
    own_rows_ref,
    own_units_ref,
    send_sem,
    recv_sem,
    local_sem,
    params_send_sem,
    params_recv_sem,
    load_sem,
    out_sem,
):
    length, width = tokens_ref.shape
    groups = width // GROUP
    blocks = full_fc_ref.shape[0]
    place = Place(shards)
    others = place.others()
    own = [group_ref.at[g] for g in range(groups)] + [own_rows_ref]
    full = [weights_ref.at[g] for g in range(groups)] + [full_out_ref]
    for number in range(blocks):
        own += [own_block_ref.at[number], own_units_ref.at[number * 128 : number * 128 + 128]]
        full += [full_fc_ref.at[number], full_proj_ref.at[number]]
    gather = Gather(place, own, full, send_sem, recv_sem, local_sem)

    def move(source, target, number):
        pltpu.make_async_copy(source, target, load_sem.at[number]).start()

    def moved(whole, number):
        pltpu.make_async_copy(whole, whole, load_sem.at[number]).wait()

    for g in range(groups):
        for part in range(3):
            start = part * width + g * GROUP
            move(
                own_qkv_ref.at[:, start : start + GROUP],
                group_ref.at[g, :, part * GROUP : (part + 1) * GROUP],
                g,
            )
    for number in range(blocks):
        take_block(
            move, own_fc_ref, number, shards, own_block_ref.at[number], groups + number
        )
    move(own_out_ref, own_rows_ref, groups + blocks)
    move(own_proj_ref.at[0 : blocks * 128], own_units_ref, groups + blocks + 1)
    place.meet([place.peer(*other) for other in others] + [place.across(), place.sibling()])

    def table(number, other, arriving):
        target = tables_ref.at[place.shard(*other) if arriving else place.me]
        return remote(
            target if arriving else own_params_ref,
            target,
            params_send_sem.at[number],
            params_recv_sem.at[number],
            place.peer(*other),
        )

    for number, other in enumerate(others):
        table(number, other, False).start()
    runner = Runner(FORWARD_PLAN, gather, ())

    def outward(g):
        return (
            pltpu.make_async_copy(held_ref.at[g], projected_ref.at[g], out_sem.at[g, 0]),
            pltpu.make_async_copy(weights_ref.at[g], full_qkv_ref.at[g], out_sem.at[g, 1]),
        )

    for g in range(groups):
        moved(group_ref.at[g], g)
        runner.act([event for event in FORWARD_PLAN[P0] if event[1] == g])
    moved(own_rows_ref, groups + blocks)
    moved(own_units_ref, groups + blocks + 1)
    runner.act([event for event in FORWARD_PLAN[P0] if event[1] >= groups])
    for g in range(groups):
        gather.keep(g).start()
    for number in range(blocks):
        moved(own_block_ref.at[number], groups + number)
    for at in range(groups, groups + 1 + 2 * blocks):
        gather.keep(at).start()
    tables_ref[place.me] = own_params_ref[...]
    build_mask(segment_ref, mask_ref)
    runner.do(P1)
    for number, other in enumerate(others):
        table(number, other, True).wait_recv()
    spread_params(shards, width // shards, tables_ref, params_ref)
    first_norm(tokens_ref, params_ref, normed_ref)
    runner.do(P2)

    @pl.loop(0, 2 * groups)
    def _(pair):
        g, odd = pair // 2, pair % 2
        runner.at_step(pair, NEED)

        @pl.when(odd == 0)
        def _():
            part = block(g, GROUP)
            weights = weights_ref[g].reshape(width, 3 * GROUP)
            values = matmul(normed_ref[...], weights, NN)
            bias = jnp.concatenate(
                [
                    params_ref[BIAS_Q : BIAS_Q + 1, part],
                    jnp.zeros((1, GROUP), f32),
                    params_ref[BIAS_V : BIAS_V + 1, part],
                ],
                axis=1,
            )
            held_ref[g] = (values + bias).astype(bf16)
            values_t_ref[part, :] = jnp.transpose(held_ref[g, :, 2 * GROUP :])
            for copy in outward(g):
                copy.start()

        attend_forward(
            pair,
            held_ref[g, :, block(odd, 2 * HEAD)],
            held_ref[g, :, block(2 + odd, 2 * HEAD)],
            values_t_ref,
            mask_ref,
            attended_t_ref,
            lse_ref,
            lambda which: runner.at_step(pair, which),
        )

    runner.do(END)
    for g in range(groups):
        for copy in outward(g):
            copy.wait()
    for at in range(groups + 1 + 2 * blocks):
        gather.drain(at)
    for number, other in enumerate(others):
        table(number, other, False).wait_send()


def spread_params(shards, own, tables_ref, params_ref):
    span = params_ref.shape[1]
    lane = lax.broadcasted_iota(jnp.int32, (128, span), 0)
    column = lax.broadcasted_iota(jnp.int32, (128, span), 1)
    narrow = wide = 0.0
    for shard in range(shards):
        values = tables_ref[shard]
        place = (column == lane + shard * own) & (lane < own)
        narrow = narrow + matmul(values, place.astype(f32).astype(bf16), NN)
        place = column == lane + shard * 128
        wide = wide + matmul(values, place.astype(f32).astype(bf16), NN)
    params_ref[0:8] = narrow[0:8]
    params_ref[8:16] = wide[8:16]


def take_block(move, own_fc_ref, number, shards, target_ref, sem):
    own = own_fc_ref.shape[1] // shards
    for shard in range(shards):
        start = shard * own + number * 128
        move(
            own_fc_ref.at[:, start : start + 128],
            target_ref.at[:, shard * 128 : (shard + 1) * 128],
            sem,
        )


def hidden_kernel(
    attended_t_ref,
    tokens_ref,
    cotangent_ref,
    params_ref,
    w_out_ref,
    w_fc_ref,
    w_proj_ref,
    layer_out_ref,
    grad_middle_ref,
    grad_attended_ref,
    grad_w_out_ref,
    grad_w_fc_ref,
    grad_w_proj_t_ref,
    small_ref,
    middle_ref,
    normed_ref,
    normed_t_ref,
    cotangent_t_ref,
    mixed_ref,
    grad_normed_ref,
    activated_ref,
    grad_preact_ref,
):
    step, steps = pl.program_id(0), pl.num_programs(0)
    length, width = tokens_ref.shape
    row = lambda at: params_ref[at : at + 1, :]
    chunks = [slice(at, at + ROW_CHUNK) for at in range(0, length, ROW_CHUNK)]

    @pl.when(step == 0)
    def _():
        attended = jnp.transpose(attended_t_ref[...])
        middle_ref[...] = (
            tokens_ref[...].astype(f32) + matmul(attended, w_out_ref[...], NN) + row(BIAS_OUT)
        )
        for rows in chunks:
            norm, _ = normalized(middle_ref[rows])
            normed_ref[rows] = (norm * row(GAIN2) + row(SHIFT2)).astype(bf16)
        normed_t_ref[...] = jnp.transpose(normed_ref[...])
        cotangent_t_ref[...] = jnp.transpose(cotangent_ref[...])
        mixed_ref[...] = jnp.zeros_like(mixed_ref)
        grad_normed_ref[...] = jnp.zeros_like(grad_normed_ref)
        small_ref[...] = jnp.zeros_like(small_ref)

    bias_sum = 0.0
    bias_row = params_ref[pl.ds(BIAS_FC + step, 1), :]
    for rows in chunks:
        preact = matmul(normed_ref[rows], w_fc_ref[...], NN) + bias_row
        grad_act = matmul(cotangent_ref[rows], w_proj_ref[...], NT)
        square = preact * preact
        bend = jnp.tanh(GELU_SCALE * preact * (1.0 + GELU_CUBE * square))
        gate = 0.5 + 0.5 * bend
        activated_ref[rows] = (preact * gate).astype(bf16)
        slope = gate + (0.5 * GELU_SCALE) * preact * (1.0 - bend * bend) * (
            1.0 + (3 * GELU_CUBE) * square
        )
        grad_preact = (slope * grad_act).astype(bf16)
        grad_preact_ref[rows] = grad_preact
        bias_sum = bias_sum + total(grad_preact.astype(f32))
    small_ref[pl.ds(BIAS_FC + step, 1), :] = bias_sum
    mixed_ref[...] += matmul(activated_ref[...], w_proj_ref[...], NN)
    grad_w_proj_t = matmul(cotangent_t_ref[...], activated_ref[...], NN).astype(bf16)
    pieces, _, piece = grad_w_proj_t_ref.shape
    for at in range(pieces):
        grad_w_proj_t_ref[at] = grad_w_proj_t[:, at * piece : (at + 1) * piece]
    grad_w_fc_ref[...] = matmul(normed_t_ref[...], grad_preact_ref[...], NN).astype(bf16)
    grad_normed_ref[...] += matmul(grad_preact_ref[...], w_fc_ref[...], NT)

    @pl.when(step == steps - 1)
    def _():
        sums = [0.0] * 4
        for rows in chunks:
            middle = middle_ref[rows]
            layer_out_ref[rows] = (middle + mixed_ref[rows] + row(BIAS_PROJ)).astype(bf16)
            norm, inverse = normalized(middle)
            grad_normed = grad_normed_ref[rows]
            cotangent = cotangent_ref[rows].astype(f32)
            grad_middle = cotangent + norm_pull(grad_normed, row(GAIN2), norm, inverse)
            grad_middle_ref[rows] = grad_middle
            normed_ref[rows] = grad_middle.astype(bf16)
            terms = (grad_middle, grad_normed * norm, grad_normed, cotangent)
            sums = [a + total(b) for a, b in zip(sums, terms)]
        for at, value in zip((BIAS_OUT, GAIN2, SHIFT2, BIAS_PROJ), sums):
            small_ref[at : at + 1, :] = value
        grad_branch = normed_ref[...]
        grad_w_out_ref[...] = matmul(attended_t_ref[...], grad_branch, NN).astype(bf16)
        grad_attended_ref[...] = matmul(grad_branch, w_out_ref[...], NT).astype(bf16)


def sum_hidden_kernel(
    shards,
    attended_t_in_ref,
    tokens_in_ref,
    cotangent_in_ref,
    params_ref,
    w_out_in_ref,
    fc_in_ref,
    proj_in_ref,
    own_fc_ref,
    own_proj_ref,
    layer_out_ref,
    grad_middle_ref,
    grad_attended_ref,
    grad_out_ref,
    last_fc_ref,
    last_proj_ref,
    done_fc_ref,
    done_proj_ref,
    small_ref,
    middle_ref,
    normed_ref,
    normed_t_ref,
    cotangent_t_ref,
    mixed_ref,
    grad_normed_ref,
    activated_ref,
    grad_preact_ref,
    fc_ref,
    proj_ref,
    grad_fc_ref,
    grad_proj_ref,
    own_block_ref,
    attended_t_ref,
    tokens_ref,
    cotangent_ref,
    w_out_ref,
    layer_ref,
    *rest,
):
    length, width = tokens_ref.shape
    blocks = fc_ref.shape[0]
    units = fc_ref.shape[3]
    early = fc_in_ref.shape[0]
    summed = done_fc_ref.shape[0]
    buffers, rest = [rest[SUM_BUFFERS * k :][:SUM_BUFFERS] for k in range(2 * summed)], rest[
        SUM_BUFFERS * 2 * summed :
    ]
    send_sem, recv_sem, local_sem, load_sem, sum_send_sem, sum_recv_sem = rest
    row = lambda at: params_ref[at : at + 1, 0:width]
    chunks = [slice(at, at + ROW_CHUNK) for at in range(0, length, ROW_CHUNK)]
    place = Place(shards)

    def move(source, target, number):
        pltpu.make_async_copy(source, target, load_sem.at[number]).start()

    def moved(whole, number):
        pltpu.make_async_copy(whole, whole, load_sem.at[number]).wait()

    own, full = [], []
    for number in range(early, blocks):
        own_block = own_block_ref.at[number - early]
        take_block(move, own_fc_ref, number, shards, own_block, number)
        own += [own_block, own_proj_ref.at[number * 128 : number * 128 + 128]]
        full += [fc_ref.at[number], proj_ref.at[number]]
    inputs = (
        (attended_t_in_ref, attended_t_ref),
        (w_out_in_ref, w_out_ref),
        (tokens_in_ref, tokens_ref),
        (cotangent_in_ref, cotangent_ref),
    )
    for number, pair in enumerate(inputs):
        move(*pair, 2 * blocks + number)
    for number in range(early):
        move(fc_in_ref.at[number], fc_ref.at[number], number)
        move(proj_in_ref.at[number], proj_ref.at[number], blocks + number)
    gather = Gather(place, own, full, send_sem, recv_sem, local_sem)
    sums = []
    for number in range(summed):
        for grad, done in ((grad_proj_ref, done_proj_ref), (grad_fc_ref, done_fc_ref)):
            k = len(sums)
            sums.append(
                Summed(
                    place,
                    grad.at[number],
                    done.at[number],
                    buffers[k],
                    sum_send_sem.at[k],
                    sum_recv_sem.at[k],
                )
            )
    runner = Runner(HIDDEN_PLAN, gather, sums)
    place.meet(
        [place.peer(hop, 0) for hop in range(1, place.lines)]
        + [place.peer(0, 1), place.across(), place.sibling()]
    )
    for number in range(early, blocks):
        moved(own_block_ref.at[number - early], number)
    runner.do(H0)
    for at in range(len(own)):
        gather.keep(at).start()

    for number, pair in enumerate(inputs):
        moved(pair[1], 2 * blocks + number)
    attended = jnp.transpose(attended_t_ref[...])
    w_out = w_out_ref[...].reshape(width, width)
    middle_ref[...] = tokens_ref[...].astype(f32) + matmul(attended, w_out, NN) + row(BIAS_OUT)
    runner.do(H1)

    @pl.loop(0, len(chunks))
    def _(number):
        norm, _ = normalized(middle_ref[chunk(number)])
        normed_ref[chunk(number)] = (norm * row(GAIN2) + row(SHIFT2)).astype(bf16)

    runner.do(H2)
    normed_t_ref[...] = jnp.transpose(normed_ref[...])
    cotangent_t_ref[...] = jnp.transpose(cotangent_ref[...])
    mixed_ref[...] = jnp.zeros_like(mixed_ref)
    grad_normed_ref[...] = jnp.zeros_like(grad_normed_ref)
    small_ref[...] = jnp.zeros_like(small_ref)
    for number in range(early):
        moved(fc_ref.at[number], number)
        moved(proj_ref.at[number], blocks + number)
    runner.do(H3)

    table = {
        step * len(chunks) + tick: events
        for tick in range(len(chunks))
        for step, events in HIDDEN_PLAN.get(tick, {}).items()
    }

    @pl.loop(0, blocks)
    def _(step):
        runner.at_step(step, NEED)
        w_fc = fc_ref.at[step]
        w_proj = proj_ref.at[step]
        bias_row = params_ref[pl.ds(BIAS_FC + step, 1), 0:units]

        @pl.loop(0, len(chunks))
        def _(number):
            runner.on(step * len(chunks) + number, table)
            rows = chunk(number)
            preact = matmul(normed_ref[rows], w_fc[...].reshape(width, units), NN) + bias_row
            grad_act = matmul(cotangent_ref[rows], w_proj[...].reshape(units, width), NT)
            square = preact * preact
            bend = jnp.tanh(GELU_SCALE * preact * (1.0 + GELU_CUBE * square))
            gate = 0.5 + 0.5 * bend
            activated_ref[rows] = (preact * gate).astype(bf16)
            slope = gate + (0.5 * GELU_SCALE) * preact * (1.0 - bend * bend) * (
                1.0 + (3 * GELU_CUBE) * square
            )
            grad_preact = (slope * grad_act).astype(bf16)
            grad_preact_ref[rows] = grad_preact
            small_ref[pl.ds(BIAS_FC + step, 1), 0:units] += total(grad_preact.astype(f32))

        runner.at_step(step, len(chunks))
        grad_proj = matmul(cotangent_t_ref[...], activated_ref[...], NN).astype(bf16)
        for shard in range(shards):
            grad_proj_ref[step, shard] = grad_proj[:, shard * 128 : (shard + 1) * 128]
        runner.at_step(step, len(chunks) + 1)
        grad_fc = matmul(normed_t_ref[...], grad_preact_ref[...], NN).astype(bf16)
        grad_fc_ref[step] = grad_fc.reshape(grad_fc_ref.shape[1:])
        runner.at_step(step, len(chunks) + 2)
        mixed_ref[...] += matmul(activated_ref[...], w_proj[...].reshape(units, width), NN)
        runner.at_step(step, len(chunks) + 3)
        grad_normed_ref[...] += matmul(
            grad_preact_ref[...], w_fc[...].reshape(width, units), NT
        )

    hand_over = []

    def hand(source, target):
        copy = pltpu.make_async_copy(source, target, load_sem.at[len(hand_over)])
        copy.start()
        hand_over.append(copy)

    hand(grad_fc_ref.at[summed:blocks], last_fc_ref)
    hand(grad_proj_ref.at[summed:blocks], last_proj_ref)
    runner.do(E0)

    @pl.loop(0, len(chunks))
    def _(number):
        rows = chunk(number)
        middle = middle_ref[rows]
        layer_ref[rows] = (middle + mixed_ref[rows] + row(BIAS_PROJ)).astype(bf16)
        norm, inverse = normalized(middle)
        grad_normed = grad_normed_ref[rows]
        cotangent = cotangent_ref[rows].astype(f32)
        grad_middle = cotangent + norm_pull(grad_normed, row(GAIN2), norm, inverse)
        middle_ref[rows] = grad_middle
        normed_ref[rows] = grad_middle.astype(bf16)
        terms = (grad_middle, grad_normed * norm, grad_normed, cotangent)
        for at, term in zip((BIAS_OUT, GAIN2, SHIFT2, BIAS_PROJ), terms):
            small_ref[at : at + 1, 0:width] += total(term)

    runner.do(E1)
    hand(middle_ref, grad_middle_ref)
    hand(layer_ref, layer_out_ref)
    runner.do(E2)
    grad_branch = normed_ref[...]
    grad_out = matmul(attended_t_ref[...], grad_branch, NN).astype(bf16)
    grad_out_ref[...] = grad_out.reshape(grad_out_ref.shape)
    runner.do(E3)
    grad_attended_ref[...] = matmul(grad_branch, w_out, NT).astype(bf16)
    runner.do(END)
    for copy in hand_over:
        copy.wait()
    for item in sums:
        item.drain()
    for at in range(len(own)):
        gather.drain(at)


def backward_kernel(
    tokens_ref,
    segment_ref,
    params_ref,
    w_qkv_ref,
    projected_ref,
    attended_t_ref,
    lse_ref,
    grad_attended_ref,
    grad_middle_ref,
    small_in_ref,
    grad_tokens_ref,
    grad_w_qkv_ref,
    small_ref,
    mask_ref,
    wide_t_ref,
    grad_queries_t_ref,
    dots_ref,
    grad_projected_ref,
    grad_keys_ref,
    grad_values_ref,
):
    length, width = tokens_ref.shape
    build_mask(segment_ref, mask_ref)
    dot_rows(attended_t_ref, grad_attended_ref, wide_t_ref, dots_ref)
    wide_t_ref[...] = jnp.transpose(projected_ref[:, width : 2 * width])

    pairs = width // (2 * HEAD)

    @pl.loop(0, pairs)
    def _(pair):
        parts = [projected_ref[:, block(k * pairs + pair, 2 * HEAD)] for k in range(3)]
        attend_backward(
            pair,
            parts + [grad_attended_ref[:, block(pair, 2 * HEAD)]],
            wide_t_ref,
            mask_ref,
            lse_ref,
            dots_ref,
            grad_queries_t_ref,
            grad_keys_ref,
            grad_values_ref,
        )
        for k, ref in ((1, grad_keys_ref), (2, grad_values_ref)):
            grad_projected_ref[:, block(k * pairs + pair, 2 * HEAD)] = ref[...].astype(bf16)

    grad_projected_ref[:, 0:width] = jnp.transpose(grad_queries_t_ref[...])
    normed_transposed(tokens_ref, params_ref, wide_t_ref)
    small_ref[...] = small_in_ref[...]
    bias_sums(grad_projected_ref, small_ref)
    grad_w_qkv_ref[...] = matmul(wide_t_ref[...], grad_projected_ref[...], NN).astype(bf16)
    gain_sum = shift_sum = 0.0
    for at in range(0, length, ROW_CHUNK):
        gain_part, shift_part = token_rows(
            slice(at, at + ROW_CHUNK),
            tokens_ref,
            params_ref,
            matmul(grad_projected_ref[at : at + ROW_CHUNK], w_qkv_ref[...], NT),
            grad_middle_ref[at : at + ROW_CHUNK],
            grad_tokens_ref,
        )
        gain_sum, shift_sum = gain_sum + gain_part, shift_sum + shift_part
    small_ref[GAIN1 : GAIN1 + 1, :] = gain_sum
    small_ref[SHIFT1 : SHIFT1 + 1, :] = shift_sum


def dot_rows(attended_t_ref, grad_attended_ref, wide_t_ref, dots_ref):
    wide_t_ref[...] = jnp.transpose(grad_attended_ref[...])
    for head in range(wide_t_ref.shape[0] // HEAD):
        rows = slice(head * HEAD, (head + 1) * HEAD)
        dots_ref[head : head + 1, :] = total(
            wide_t_ref[rows].astype(f32) * attended_t_ref[rows].astype(f32)
        )


def normed_transposed(tokens_ref, params_ref, wide_t_ref):
    width = tokens_ref.shape[1]
    row = lambda at: params_ref[at : at + 1, 0:width]

    @pl.loop(0, tokens_ref.shape[0] // ROW_CHUNK)
    def _(number):
        norm, _ = normalized(tokens_ref[chunk(number)].astype(f32))
        normed = (norm * row(GAIN1) + row(SHIFT1)).astype(bf16)
        wide_t_ref[:, chunk(number)] = jnp.transpose(normed)


def bias_sums(grad_projected_ref, small_ref):
    width = small_ref.shape[1]
    for at, part in ((BIAS_Q, 0), (BIAS_V, 2)):
        values = grad_projected_ref[:, part * width : (part + 1) * width]
        small_ref[at : at + 1, :] = total(values.astype(f32))


def token_rows(rows, tokens_ref, params_ref, grad_normed, middle, grad_tokens_ref):
    gain = params_ref[GAIN1 : GAIN1 + 1, 0 : tokens_ref.shape[1]]
    norm, inverse = normalized(tokens_ref[rows].astype(f32))
    grad_rows = norm_pull(grad_normed, gain, norm, inverse)
    grad_tokens_ref[rows] = (middle + grad_rows).astype(bf16)
    return total(grad_normed * norm), total(grad_normed)


def sum_backward_kernel(
    shards,
    tokens_in_ref,
    segment_ref,
    params_ref,
    attended_t_in_ref,
    lse_ref,
    grad_attended_in_ref,
    small_in_ref,
    projected_in_ref,
    w_qkv_in_ref,
    grad_middle_in_ref,
    grad_out_in_ref,
    grad_fc_in_ref,
    grad_proj_in_ref,
    grad_tokens_ref,
    done_qkv_ref,
    done_out_ref,
    done_fc_ref,
    done_proj_ref,
    own_small_ref,
    mask_ref,
    wide_t_ref,
    normed_t_ref,
    grad_queries_t_ref,
    dots_ref,
    projected_ref,
    grad_projected_ref,
    grad_keys_ref,
    grad_values_ref,
    grad_qkv_ref,
    grad_out_ref,
    grad_fc_ref,
    grad_proj_ref,
    weights_ref,
    tokens_ref,
    attended_t_ref,
    grad_attended_ref,
    *rest,
):
    length, width = tokens_ref.shape
    groups = width // GROUP
    late_blocks = grad_fc_ref.shape[0]
    items = 2 * late_blocks + 1 + groups
    buffers, rest = [rest[SUM_BUFFERS * k :][:SUM_BUFFERS] for k in range(items)], rest[
        SUM_BUFFERS * items :
    ]
    small_ref, parts_ref, core_parts_ref, far_parts_ref, side_parts_ref, line_parts_ref, *rest = rest
    send_sem, recv_sem, load_sem, small_send_sem, small_recv_sem = rest
    place = Place(shards)
    lines = place.lines
    arrays = []
    for number in range(late_blocks):
        arrays += [
            (grad_proj_ref.at[number], done_proj_ref.at[number], grad_proj_in_ref.at[number]),
            (grad_fc_ref.at[number], done_fc_ref.at[number], grad_fc_in_ref.at[number]),
        ]
    arrays.append((grad_out_ref, done_out_ref, grad_out_in_ref))
    arrays += [(grad_qkv_ref.at[g], done_qkv_ref.at[g], None) for g in range(groups)]
    sums = [
        Summed(
            place,
            grad,
            done,
            buffers[k],
            send_sem.at[k],
            recv_sem.at[k],
            source,
            None if source is None else load_sem.at[k],
        )
        for k, (grad, done, source) in enumerate(arrays)
    ]
    runner = Runner(BACKWARD_PLAN, None, sums)
    load_projected = pltpu.make_async_copy(projected_in_ref, projected_ref, load_sem.at[items])
    load_projected.start()
    inputs = [
        pltpu.make_async_copy(source, target, load_sem.at[items + 2 + number])
        for number, (source, target) in enumerate(
            (
                (attended_t_in_ref, attended_t_ref),
                (grad_attended_in_ref, grad_attended_ref),
                (tokens_in_ref, tokens_ref),
            )
        )
    ]
    for copy in inputs:
        copy.start()
    load_weights = pltpu.make_async_copy(w_qkv_in_ref, weights_ref, load_sem.at[items + 1])
    load_weights.start()
    place.meet(
        [place.peer(hop, 0) for hop in range(1, lines)]
        + [place.peer(0, 1), place.across(), place.sibling()]
    )
    runner.do(B0)
    build_mask(segment_ref, mask_ref)
    runner.do(B1)
    for copy in inputs:
        copy.wait()
    dot_rows(attended_t_ref, grad_attended_ref, wide_t_ref, dots_ref)
    runner.do(B2)
    normed_transposed(tokens_ref, params_ref, normed_t_ref)
    small_ref[...] = small_in_ref[...]
    parts_ref[...] = jnp.zeros_like(parts_ref)
    load_projected.wait()
    for g in range(groups):
        wide_t_ref[g * GROUP : (g + 1) * GROUP] = jnp.transpose(
            projected_ref[g, :, GROUP : 2 * GROUP]
        )
    runner.do(B3)

    @pl.loop(0, 2 * groups)
    def _(pair):
        g, odd = pair // 2, pair % 2
        parts = [projected_ref[g, :, block(2 * k + odd, 2 * HEAD)] for k in range(3)]
        attend_backward(
            pair,
            parts + [grad_attended_ref[:, block(pair, 2 * HEAD)]],
            wide_t_ref,
            mask_ref,
            lse_ref,
            dots_ref,
            grad_queries_t_ref,
            grad_keys_ref,
            grad_values_ref,
            lambda number: runner.at_step(pair, number),
        )
        grad_queries = jnp.transpose(grad_queries_t_ref[block(pair, 2 * HEAD), :])
        grad_projected_ref[g, :, block(odd, 2 * HEAD)] = grad_queries
        for k, ref in ((1, grad_keys_ref), (2, grad_values_ref)):
            grad_projected_ref[g, :, block(2 * k + odd, 2 * HEAD)] = ref[...].astype(bf16)

        @pl.when(odd == 1)
        def _():
            grad_group = matmul(normed_t_ref[...], grad_projected_ref[g], NN).astype(bf16)
            grad_qkv_ref[g] = grad_group.reshape(grad_qkv_ref.shape[1:])

    middle_ref = mask_ref.at[:, 0:width]
    load_middle = pltpu.make_async_copy(grad_middle_in_ref, middle_ref, load_sem.at[items])
    load_middle.start()
    for g in range(groups):
        part = slice(g * GROUP, (g + 1) * GROUP)
        for at, k in ((BIAS_Q, 0), (BIAS_V, 2)):
            values = grad_projected_ref[g, :, k * GROUP : (k + 1) * GROUP]
            small_ref[at : at + 1, part] = total(values.astype(f32))
    load_weights.wait()
    load_middle.wait()
    table = {k: BACKWARD_PLAN.get(E0 + k, ()) for k in range(length // ROW_CHUNK)}

    @pl.loop(0, length // ROW_CHUNK)
    def _(number):
        runner.on(number, table)
        rows = chunk(number)
        grad_normed = 0.0
        for g in range(groups):
            weights = weights_ref[g].reshape(width, 3 * GROUP)
            grad_normed = grad_normed + matmul(grad_projected_ref[g, rows], weights, NT)
        gain_part, shift_part = token_rows(
            rows, tokens_ref, params_ref, grad_normed, mask_ref[rows, 0:width], grad_tokens_ref
        )
        small_ref[GAIN1 : GAIN1 + 1, 0:width] += gain_part
        small_ref[SHIFT1 : SHIFT1 + 1, 0:width] += shift_part

    own = width // shards
    for shard in range(shards):
        into = parts_ref.at[shard // 2, shard % 2]
        into[0:8, 0:own] = small_ref[0:8, shard * own : (shard + 1) * own]
        into[8:16, :] = small_ref[8:16, shard * 128 : (shard + 1) * 128]

    def exchange(slot, source, into, peer):
        copy = remote(source, into, small_send_sem.at[slot], small_recv_sem.at[slot], peer)
        copy.start()
        return copy

    line, side = place.line, place.side
    todo = BACKWARD_PLAN.get(END, ())
    portions = [todo[len(todo) * k // 5 : len(todo) * (k + 1) // 5] for k in range(5)]
    copy = exchange(0, parts_ref, core_parts_ref, place.sibling())
    runner.act(portions[0])
    copy.wait()
    parts_ref[...] += core_parts_ref[...]
    copy = exchange(1, parts_ref, far_parts_ref, place.across())
    runner.act(portions[1])
    copy.wait()
    parts_ref[...] += far_parts_ref[...]
    copy = exchange(2, parts_ref.at[:, 1 - side], side_parts_ref, place.peer(0, 1))
    runner.act(portions[2])
    copy.wait()
    parts_ref[:, side] += side_parts_ref[...]
    copies = [
        exchange(
            2 + hop,
            parts_ref.at[flip(line, hop), side],
            line_parts_ref.at[hop - 1],
            place.peer(hop, 0),
        )
        for hop in range(1, lines)
    ]
    runner.act(portions[3] + portions[4])
    for copy in copies:
        copy.wait()
    small = parts_ref[line, side]
    for hop in range(1, lines):
        small = small + line_parts_ref[hop - 1]
    own_small_ref[...] = small
    for item in sums:
        item.drain()


def finish_kernel(
    shards,
    qkv_ref,
    out_ref,
    fc_early_ref,
    fc_last_ref,
    proj_early_ref,
    proj_last_ref,
    small_ref,
    layer_in_ref,
    tokens_in_ref,
    sum_qkv_ref,
    sum_out_ref,
    sum_fc_ref,
    sum_proj_ref,
    layer_out_ref,
    grad_tokens_ref,
    *rest,
):
    *vector_refs, fc_bias_ref, copy_sem = rest
    copies = [
        pltpu.make_async_copy(source, target, copy_sem.at[k])
        for k, (source, target) in enumerate(
            ((layer_in_ref, layer_out_ref), (tokens_in_ref, grad_tokens_ref))
        )
    ]
    for copy in copies:
        copy.start()
    groups, own, _ = qkv_ref.shape
    width = groups * GROUP
    for g in range(groups):
        for part in range(3):
            start = part * width + g * GROUP
            sum_qkv_ref[:, start : start + GROUP] = qkv_ref[
                g, :, part * GROUP : (part + 1) * GROUP
            ].astype(f32)
    sum_out_ref[...] = out_ref[...].astype(f32)
    early = fc_early_ref.shape[0]
    blocks = early + fc_last_ref.shape[0]
    for number in range(blocks):
        fc = fc_early_ref.at[number] if number < early else fc_last_ref.at[number - early]
        proj = proj_early_ref.at[number] if number < early else proj_last_ref.at[number - early]
        for shard in range(shards):
            start = (shard * blocks + number) * 128
            sum_fc_ref[:, start : start + 128] = fc[:, shard * 128 : (shard + 1) * 128].astype(f32)
        sum_proj_ref[number * 128 : (number + 1) * 128] = jnp.transpose(proj[...].astype(f32))
    for at, vector_ref in enumerate(vector_refs):
        vector_ref[...] = small_ref[at, 0:own]
    for number in range(blocks):
        fc_bias_ref[number * 128 : (number + 1) * 128] = small_ref[BIAS_FC + number, :]
    for copy in copies:
        copy.wait()


def kernel_params():
    return pltpu.CompilerParams(vmem_limit_bytes=VMEM_LIMIT)


def run_forward(tokens, segment, params, w_qkv):
    length, width = tokens.shape
    return pl.pallas_call(
        forward_kernel,
        in_specs=[WHOLE] * 4,
        out_specs=(WHOLE,) * 3,
        out_shape=(
            jax.ShapeDtypeStruct((length, 3 * width), bf16),
            jax.ShapeDtypeStruct((width, length), bf16),
            jax.ShapeDtypeStruct((16, length), f32),
        ),
        scratch_shapes=[
            pltpu.VMEM((length, length), f32),
            pltpu.VMEM((length, width), bf16),
            pltpu.VMEM((width, length), bf16),
        ],
        compiler_params=kernel_params(),
        name="forward",
    )(tokens, segment, params, w_qkv)


def run_hidden(attended_t, tokens, cotangent, params, w_out, w_fc, w_proj, piece):
    length, width = tokens.shape
    hidden = w_fc.shape[1]
    shape = jax.ShapeDtypeStruct
    columns = pl.BlockSpec((width, width), lambda step: (0, step))
    return pl.pallas_call(
        hidden_kernel,
        grid=(hidden // width,),
        in_specs=[WHOLE] * 5 + [columns, pl.BlockSpec((width, width), lambda step: (step, 0))],
        out_specs=(
            WHOLE,
            WHOLE,
            WHOLE,
            WHOLE,
            columns,
            pl.BlockSpec((width // piece, width, piece), lambda step: (step, 0, 0)),
            WHOLE,
        ),
        out_shape=(
            shape((length, width), bf16),
            shape((length, width), f32),
            shape((length, width), bf16),
            shape((width, width), bf16),
            shape((width, hidden), bf16),
            shape((hidden // piece, width, piece), bf16),
            shape((16, width), f32),
        ),
        scratch_shapes=[
            pltpu.VMEM((length, width), f32),
            pltpu.VMEM((length, width), bf16),
            pltpu.VMEM((width, length), bf16),
            pltpu.VMEM((width, length), bf16),
            pltpu.VMEM((length, width), f32),
            pltpu.VMEM((length, width), f32),
            pltpu.VMEM((length, width), bf16),
            pltpu.VMEM((length, width), bf16),
        ],
        compiler_params=kernel_params(),
        name="hidden",
    )(attended_t, tokens, cotangent, params, w_out, w_fc, w_proj)


def run_backward(
    tokens, segment, params, w_qkv, projected, attended_t, lse, grad_attended, grad_middle, small
):
    length, width = tokens.shape
    shape = jax.ShapeDtypeStruct
    return pl.pallas_call(
        backward_kernel,
        in_specs=[WHOLE] * 10,
        out_specs=(WHOLE,) * 3,
        out_shape=(
            shape((length, width), bf16),
            shape((width, 3 * width), bf16),
            shape((16, width), f32),
        ),
        scratch_shapes=[
            pltpu.VMEM((length, length), f32),
            pltpu.VMEM((width, length), bf16),
            pltpu.VMEM((width, length), bf16),
            pltpu.VMEM((16, length), f32),
            pltpu.VMEM((length, 3 * width), bf16),
            pltpu.VMEM((length, 2 * HEAD), f32),
            pltpu.VMEM((length, 2 * HEAD), f32),
        ],
        compiler_params=kernel_params(),
        name="backward",
    )(
        tokens,
        segment,
        params,
        w_qkv,
        projected,
        attended_t,
        lse,
        grad_attended,
        grad_middle,
        small,
    )


def link_params(number):
    return pltpu.CompilerParams(
        vmem_limit_bytes=VMEM_LIMIT, collective_id=number, has_side_effects=True
    )


def run_gather_forward(
    shards, span, tokens, segment, own_params, w_qkv, w_out, w_fc, w_proj
):
    length, width = tokens.shape
    own = w_qkv.shape[0]
    groups = width // GROUP
    blocks = GATHERED_EARLY
    items = groups + 1 + 2 * blocks
    shape = jax.ShapeDtypeStruct
    copies = 3 * shards - 3
    dma = pltpu.SemaphoreType.DMA
    return pl.pallas_call(
        partial(gather_forward_kernel, shards),
        in_specs=[WHOLE] * 3 + [HBM] * 4,
        out_specs=(HBM,) + (WHOLE,) * 3 + (HBM,) * 4,
        out_shape=(
            shape((groups, length, 3 * GROUP), bf16),
            shape((width, length), bf16),
            shape((16, length), f32),
            shape((own_params.shape[0], span), f32),
            shape((groups, shards, own, 3 * GROUP), bf16),
            shape((shards, own, width), bf16),
            shape((blocks, shards, own, shards * 128), bf16),
            shape((blocks, shards, 128, width), bf16),
        ),
        scratch_shapes=[
            pltpu.VMEM((length, length), f32),
            pltpu.VMEM((length, width), bf16),
            pltpu.VMEM((width, length), bf16),
            pltpu.VMEM((groups, length, 3 * GROUP), bf16),
            pltpu.VMEM((groups, shards, own, 3 * GROUP), bf16),
            pltpu.VMEM((shards,) + own_params.shape, bf16),
            pltpu.VMEM((groups, own, 3 * GROUP), bf16),
            pltpu.VMEM((blocks, own, shards * 128), bf16),
            pltpu.VMEM((own, width), bf16),
            pltpu.VMEM((blocks * 128, width), bf16),
            dma((items, copies)),
            dma((items, copies)),
            dma((items,)),
            dma((shards - 1,)),
            dma((shards - 1,)),
            dma((groups + blocks + 2,)),
            dma((groups, 2)),
        ],
        compiler_params=link_params(0),
        name="gather_forward",
    )(tokens, segment, own_params, w_qkv, w_out, w_fc, w_proj)


def run_sum_hidden(
    shards, attended_t, tokens, cotangent, params, full_out, full_fc, full_proj, w_fc, w_proj
):
    length, width = tokens.shape
    own, units = w_fc.shape[0], shards * 128
    blocks = w_proj.shape[0] // 128
    lines = shards // 2
    shape = jax.ShapeDtypeStruct
    dma = pltpu.SemaphoreType.DMA
    grads = ((shards, own, units), (shards, width, 128))
    late, early = blocks - full_fc.shape[0], SUMMED_EARLY
    buffers = [
        ref
        for _ in range(early)
        for grad in reversed(grads)
        for ref in sum_buffers(lines, *grad)
    ]
    return pl.pallas_call(
        partial(sum_hidden_kernel, shards),
        in_specs=[HBM] * 3 + [WHOLE] + [HBM] * 5,
        out_specs=(HBM, HBM, WHOLE, WHOLE, HBM, HBM) + (WHOLE,) * 3,
        out_shape=(
            shape((length, width), bf16),
            shape((length, width), f32),
            shape((length, width), bf16),
            shape((shards, own, width), bf16),
            shape((blocks - early,) + grads[0], bf16),
            shape((blocks - early,) + grads[1], bf16),
            shape((early, own, units), bf16),
            shape((early, width, 128), bf16),
            shape(params.shape, f32),
        ),
        scratch_shapes=[
            pltpu.VMEM((length, width), f32),
            pltpu.VMEM((length, width), bf16),
            pltpu.VMEM((width, length), bf16),
            pltpu.VMEM((width, length), bf16),
            pltpu.VMEM((length, width), f32),
            pltpu.VMEM((length, width), f32),
            pltpu.VMEM((length, units), bf16),
            pltpu.VMEM((length, units), bf16),
            pltpu.VMEM((blocks, shards, own, units), bf16),
            pltpu.VMEM((blocks, shards, 128, width), bf16),
            pltpu.VMEM((blocks,) + grads[0], bf16),
            pltpu.VMEM((blocks,) + grads[1], bf16),
            pltpu.VMEM((late, own, units), bf16),
            pltpu.VMEM((width, length), bf16),
            pltpu.VMEM((length, width), bf16),
            pltpu.VMEM((length, width), bf16),
            pltpu.VMEM((shards, own, width), bf16),
            pltpu.VMEM((length, width), bf16),
        ]
        + buffers
        + [
            dma((2 * late, 3 * shards - 3)),
            dma((2 * late, 3 * shards - 3)),
            dma((2 * late,)),
            dma((2 * blocks + 4,)),
        ]
        + sum_sems(lines, 2 * early),
        compiler_params=link_params(1),
        name="sum_hidden",
    )(attended_t, tokens, cotangent, params, full_out, full_fc, full_proj, w_fc, w_proj)


def run_sum_backward(
    shards,
    tokens,
    segment,
    params,
    attended_t,
    lse,
    grad_attended,
    small,
    projected,
    w_qkv,
    grad_middle,
    grad_out,
    grad_fc,
    grad_proj,
):
    length, width = tokens.shape
    shape = jax.ShapeDtypeStruct
    lines, groups = shards // 2, width // GROUP
    own = width // shards
    qkv = (shards, own, 3 * GROUP)
    late_blocks = grad_fc.shape[0]
    grads = [grad_proj.shape[1:], grad_fc.shape[1:]] * late_blocks
    grads += [grad_out.shape] + [qkv] * groups
    buffers = [ref for grad in grads for ref in sum_buffers(lines, *grad)]
    parts = pltpu.VMEM((lines, 2, 16, 128), f32)
    dma = pltpu.SemaphoreType.DMA
    items = len(grads)
    return pl.pallas_call(
        partial(sum_backward_kernel, shards),
        in_specs=[HBM, WHOLE, WHOLE, HBM, WHOLE, HBM, WHOLE] + [HBM] * 6,
        out_specs=(WHOLE,) * 6,
        out_shape=(
            shape((length, width), bf16),
            shape((groups,) + qkv[1:], bf16),
            shape(grad_out.shape[1:], bf16),
            shape((late_blocks,) + grad_fc.shape[2:], bf16),
            shape((late_blocks,) + grad_proj.shape[2:], bf16),
            shape((16, 128), f32),
        ),
        scratch_shapes=[
            pltpu.VMEM((length, length), f32),
            pltpu.VMEM((width, length), bf16),
            pltpu.VMEM((width, length), bf16),
            pltpu.VMEM((width, length), bf16),
            pltpu.VMEM((16, length), f32),
            pltpu.VMEM(projected.shape, bf16),
            pltpu.VMEM(projected.shape, bf16),
            pltpu.VMEM((length, 2 * HEAD), f32),
            pltpu.VMEM((length, 2 * HEAD), f32),
            pltpu.VMEM((groups,) + qkv, bf16),
            pltpu.VMEM(grad_out.shape, bf16),
            pltpu.VMEM(grad_fc.shape, bf16),
            pltpu.VMEM(grad_proj.shape, bf16),
            pltpu.VMEM(w_qkv.shape, bf16),
            pltpu.VMEM((length, width), bf16),
            pltpu.VMEM((width, length), bf16),
            pltpu.VMEM((length, width), bf16),
        ]
        + buffers
        + [pltpu.VMEM(params.shape, f32), parts, parts, parts]
        + [pltpu.VMEM((lines, 16, 128), f32), pltpu.VMEM((lines - 1, 16, 128), f32)]
        + sum_sems(lines, items)
        + [dma((items + 5,)), dma((lines + 2,)), dma((lines + 2,))],
        compiler_params=link_params(2),
        name="sum_backward",
    )(
        tokens,
        segment,
        params,
        attended_t,
        lse,
        grad_attended,
        small,
        projected,
        w_qkv,
        grad_middle,
        grad_out,
        grad_fc,
        grad_proj,
    )


def run_finish(
    shards, qkv, out, fc_early, fc_last, proj_early, proj_last, small, layer_out, grad_tokens
):
    groups, own, _ = qkv.shape
    width = out.shape[1]
    blocks = fc_early.shape[0] + fc_last.shape[0]
    shape = jax.ShapeDtypeStruct
    return pl.pallas_call(
        partial(finish_kernel, shards),
        in_specs=[WHOLE] * 9,
        out_specs=(WHOLE,) * 4 + (HBM,) * 2 + (WHOLE,) * 9,
        out_shape=(
            shape((own, 3 * width), f32),
            shape((own, width), f32),
            shape((own, blocks * shards * 128), f32),
            shape((blocks * 128, width), f32),
            shape(layer_out.shape, bf16),
            shape(grad_tokens.shape, bf16),
        )
        + (shape((own,), f32),) * 8
        + (shape((blocks * 128,), f32),),
        scratch_shapes=[pltpu.SemaphoreType.DMA((2,))],
        compiler_params=kernel_params(),
        name="finish",
    )(qkv, out, fc_early, fc_last, proj_early, proj_last, small, layer_out, grad_tokens)


def by_kernels(
    shards, tokens, segment_ids, vectors, fc_bias, w_qkv, w_out, w_fc, w_proj, cotangent
):
    width, hidden = tokens.shape[1], w_fc.shape[1]
    blocks, units = w_proj.shape[0] // 128, shards * 128
    span = max(width, units)
    rows = jnp.pad(jnp.stack(vectors), ((0, 0), (0, 128 - vectors[0].shape[0])))
    table = jnp.concatenate(
        [rows, jnp.pad(fc_bias.reshape(blocks, 128), ((0, 8 - blocks), (0, 0)))]
    )
    projected, attended_t, lse, params, full_qkv, full_out, full_fc, full_proj = (
        run_gather_forward(shards, span, tokens, segment_ids, table, w_qkv, w_out, w_fc, w_proj)
    )
    (
        layer_out,
        grad_middle,
        grad_attended,
        grad_out,
        grad_fc,
        grad_proj,
        fc_early,
        proj_early,
        small,
    ) = run_sum_hidden(
        shards, attended_t, tokens, cotangent, params, full_out, full_fc, full_proj, w_fc, w_proj
    )
    grad_tokens, done_qkv, done_out, fc_last, proj_last, small = run_sum_backward(
        shards,
        tokens,
        segment_ids,
        params,
        attended_t,
        lse,
        grad_attended,
        small,
        projected,
        full_qkv,
        grad_middle,
        grad_out,
        grad_fc,
        grad_proj,
    )
    sum_qkv, sum_out, sum_fc, sum_proj, layer_out, grad_tokens, *own_vectors = run_finish(
        shards,
        done_qkv,
        done_out,
        fc_early,
        fc_last,
        proj_early,
        proj_last,
        small,
        layer_out,
        grad_tokens,
    )
    pick = lambda at: own_vectors[at]
    return (
        layer_out,
        grad_tokens,
        pick(GAIN1),
        pick(SHIFT1),
        sum_qkv,
        pick(BIAS_Q),
        pick(BIAS_V),
        sum_out,
        pick(BIAS_OUT),
        pick(GAIN2),
        pick(SHIFT2),
        sum_fc,
        pick(BIAS_FC),
        sum_proj,
        pick(BIAS_PROJ),
    )


def on_device(
    replicas,
    shards,
    tokens,
    segment_ids,
    norm1_gain,
    norm1_shift,
    w_qkv,
    q_bias,
    v_bias,
    w_out,
    out_bias,
    norm2_gain,
    norm2_shift,
    w_fc,
    fc_bias,
    w_proj,
    proj_bias,
    cotangent,
):
    width, hidden = tokens.shape[1], w_fc.shape[1]
    vectors = (
        norm1_gain,
        norm1_shift,
        q_bias,
        v_bias,
        out_bias,
        norm2_gain,
        norm2_shift,
        proj_bias,
    )
    own, own_hidden = norm1_gain.shape[0], fc_bias.shape[0]
    if (
        replicas == 4
        and shards & (shards - 1) == 0
        and own % 96 == 0
        and own_hidden == 3 * 128
        and width == 3 * GROUP
    ):
        return by_kernels(
            shards, tokens, segment_ids, vectors, fc_bias, w_qkv, w_out, w_fc, w_proj, cotangent
        )
    me = lax.axis_index("shard")
    mine = (lax.broadcasted_iota(jnp.int32, (1, shards, 1), 1) == me).astype(bf16)
    table = jnp.concatenate(
        [
            (jnp.stack(vectors)[:, None, :] * mine).reshape(8, width),
            (fc_bias[None, None, :] * mine).reshape(hidden // width, width),
        ]
    )
    table = jnp.pad(table, ((0, 16 - table.shape[0]), (0, 0)))
    gather = partial(lax.all_gather, axis_name="shard", axis=0, tiled=True)
    params = lax.psum(table.astype(f32), "shard")
    full_qkv, full_out, full_fc, full_proj = (gather(w) for w in (w_qkv, w_out, w_fc, w_proj))
    projected, attended_t, lse = run_forward(tokens, segment_ids, params, full_qkv)
    (
        layer_out,
        grad_middle,
        grad_attended,
        grad_w_out,
        grad_w_fc,
        grad_w_proj_t,
        small,
    ) = run_hidden(attended_t, tokens, cotangent, params, full_out, full_fc, full_proj, width)
    grad_tokens, grad_w_qkv, small = run_backward(
        tokens,
        segment_ids,
        params,
        full_qkv,
        projected,
        attended_t,
        lse,
        grad_attended,
        grad_middle,
        small,
    )

    def reduced(grad):
        own_sum = lax.psum_scatter(grad.astype(f32), "shard", scatter_dimension=0, tiled=True)
        return lax.psum(own_sum.astype(bf16), "rep").astype(f32)

    sum_proj = reduced(grad_w_proj_t.transpose(0, 2, 1).reshape(hidden, width))
    sum_fc, sum_out, sum_qkv = reduced(grad_w_fc), reduced(grad_w_out), reduced(grad_w_qkv)
    small = lax.psum(small, ("rep", "shard"))
    mine = lax.dynamic_slice_in_dim(small[:8], me * own, own, 1)
    hidden_rows = small[BIAS_FC : BIAS_FC + hidden // width].reshape(-1)
    mine_fc = lax.dynamic_slice_in_dim(hidden_rows, me * own_hidden, own_hidden, 0)
    return (
        layer_out,
        grad_tokens,
        mine[GAIN1],
        mine[SHIFT1],
        sum_qkv,
        mine[BIAS_Q],
        mine[BIAS_V],
        sum_out,
        mine[BIAS_OUT],
        mine[GAIN2],
        mine[SHIFT2],
        sum_fc,
        mine_fc,
        sum_proj,
        mine[BIAS_PROJ],
    )


def solution(mesh):
    rows, own, own_rows = P(("rep", "shard"), None), P("shard"), P("shard", None)
    in_specs = (
        rows,
        rows,
        own,
        own,
        own_rows,
        own,
        own,
        own_rows,
        own,
        own,
        own,
        own_rows,
        own,
        own_rows,
        own,
        rows,
    )
    out_specs = (
        rows,
        rows,
        own,
        own,
        own_rows,
        own,
        own,
        own_rows,
        own,
        own,
        own,
        own_rows,
        own,
        own_rows,
        own,
    )
    sizes = mesh.shape["rep"], mesh.shape["shard"]
    return jax.shard_map(
        partial(on_device, *sizes), mesh=mesh, in_specs=in_specs, out_specs=out_specs, check_vma=False
    )
```

profile of v0, /device:TPU:0, one launch (start us, length us, event | category | flops | bytes accessed | tf_op | source)
XLA Modules:
  0.0 216.7 jit_solution(10086058762309937492)
XLA Ops:
  0.6 0.8 stack.35
  1.4 1.3 fusion.2.own_params_ref
  2.7 61.9 %gather_forward.1 = (bf16[3,1024,768]{2,1,0:T(8,128)(2,1)}, bf16[768,1024]{1,0:T(8,128)(2,1)}, f32[16,1024]{1,0:T(8,128)}, f32[16,1024]{1,0:T(8,128)}, bf16[3,8,...) custom-call(bf16[1024,768]{1,0:T(8,128)(2,1)} %tokens_in_ref.3, ...), custom_call_target="tpu_custom_call" | custom-call | tf_op jit(solution)/shard_map/gather_forward/pallas_call | solution.py:1624
  64.6 71.4 %sum_hidden.1 = (bf16[1024,768]{1,0:T(8,128)(2,1)}, f32[1024,768]{1,0:T(8,128)}, bf16[1024,768]{1,0:T(8,128)(2,1)}, bf16[8,96,768]{2,1,0:T(8,128)(2,1)}, bf16[2,...) custom-call(bf16[768,1024]{1,0:T(8,128)(2,1)} %get-tuple-element.54., ...), custom_call_target="tpu_custom_call" | custom-call | tf_op jit(solution)/shard_map/sum_hidden/pallas_call | solution.py:1679
  136.0 74.5 %sum_backward.1 = (bf16[1024,768]{1,0:T(8,128)(2,1)}, bf16[3,96,768]{2,1,0:T(8,128)(2,1)}, bf16[96,768]{1,0:T(8,128)(2,1)}, bf16[2,96,1024]{2,1,0:T(8,128)(2,1)}...) custom-call(bf16[1024,768]{1,0:T(8,128)(2,1)} %tokens_in_ref.3, s32[1,1024]{1,0:T(1,128)} %segment_ref.3, ...), custom_call_target="tpu_custom_call" | custom-call | tf_op jit(solution)/shard_map/sum_backward/pallas_call | solution.py:1755
  210.6 6.0 %finish.1 = (f32[96,2304]{1,0:T(8,128)}, f32[96,768]{1,0:T(8,128)}, f32[96,3072]{1,0:T(8,128)}, f32[384,768]{1,0:T(8,128)}, bf16[1024,768]{1,0:T(8,128)(2,1)}, /...) custom-call(bf16[3,96,768]{2,1,0:T(8,128)(2,1)} %get-tuple-element.6, ...), custom_call_target="tpu_custom_call" | custom-call | tf_op jit(solution)/shard_map/finish/pallas_call | solution.py:1817
where the time goes:
time: 217 us
  Pallas kernels  214 us (99%)
    pallas_call x1, Pallas kernels, run_sum_backward(): pl.pallas_call(partial(sum_backward_kernel, shards), in_specs=[HBM, WHOLE...  74.5 us
    pallas_call x1, Pallas kernels, run_sum_hidden(): pl.pallas_call(partial(sum_hidden_kernel, shards), in_specs=[HBM] * 3 + [...  71.4 us
    pallas_call x1, Pallas kernels, run_gather_forward(): pl.pallas_call(partial(gather_forward_kernel, shards), in_specs=[WHOLE] *...  61.9 us
    pallas_call x1, Pallas kernels, run_finish(): pl.pallas_call(partial(finish_kernel, shards), in_specs=[WHOLE] * 9, out_...  5.97 us

commit v1 on v0

--- a/solution.py
+++ b/solution.py
@@ -935,8 +935,8 @@
     own_proj_ref,
     layer_out_ref,
     grad_middle_ref,
-    grad_attended_ref,
-    grad_out_ref,
+    grad_attended_out_ref,
+    grad_out_out_ref,
     last_fc_ref,
     last_proj_ref,
     done_fc_ref,
@@ -960,6 +960,8 @@
     cotangent_ref,
     w_out_ref,
     layer_ref,
+    grad_attended_ref,
+    grad_out_ref,
     *rest,
 ):
     length, width = tokens_ref.shape
@@ -1124,8 +1126,10 @@
     grad_branch = normed_ref[...]
     grad_out = matmul(attended_t_ref[...], grad_branch, NN).astype(bf16)
     grad_out_ref[...] = grad_out.reshape(grad_out_ref.shape)
+    hand(grad_out_ref, grad_out_out_ref)
     runner.do(E3)
     grad_attended_ref[...] = matmul(grad_branch, w_out, NT).astype(bf16)
+    hand(grad_attended_ref, grad_attended_out_ref)
     runner.do(END)
     for copy in hand_over:
         copy.wait()
@@ -1251,7 +1255,7 @@
     grad_out_in_ref,
     grad_fc_in_ref,
     grad_proj_in_ref,
-    grad_tokens_ref,
+    grad_tokens_out_ref,
     done_qkv_ref,
     done_out_ref,
     done_fc_ref,
@@ -1274,6 +1278,7 @@
     tokens_ref,
     attended_t_ref,
     grad_attended_ref,
+    grad_tokens_ref,
     *rest,
 ):
     length, width = tokens_ref.shape
@@ -1398,6 +1403,8 @@
         small_ref[GAIN1 : GAIN1 + 1, 0:width] += gain_part
         small_ref[SHIFT1 : SHIFT1 + 1, 0:width] += shift_part
 
+    leave = pltpu.make_async_copy(grad_tokens_ref, grad_tokens_out_ref, load_sem.at[items])
+    leave.start()
     own = width // shards
     for shard in range(shards):
         into = parts_ref.at[shard // 2, shard % 2]
@@ -1440,6 +1447,7 @@
     for hop in range(1, lines):
         small = small + line_parts_ref[hop - 1]
     own_small_ref[...] = small
+    leave.wait()
     for item in sums:
         item.drain()
 
@@ -1679,7 +1687,7 @@
     return pl.pallas_call(
         partial(sum_hidden_kernel, shards),
         in_specs=[HBM] * 3 + [WHOLE] + [HBM] * 5,
-        out_specs=(HBM, HBM, WHOLE, WHOLE, HBM, HBM) + (WHOLE,) * 3,
+        out_specs=(HBM,) * 6 + (WHOLE,) * 3,
         out_shape=(
             shape((length, width), bf16),
             shape((length, width), f32),
@@ -1710,6 +1718,8 @@
             pltpu.VMEM((length, width), bf16),
             pltpu.VMEM((shards, own, width), bf16),
             pltpu.VMEM((length, width), bf16),
+            pltpu.VMEM((length, width), bf16),
+            pltpu.VMEM((shards, own, width), bf16),
         ]
         + buffers
         + [
@@ -1755,7 +1765,7 @@
     return pl.pallas_call(
         partial(sum_backward_kernel, shards),
         in_specs=[HBM, WHOLE, WHOLE, HBM, WHOLE, HBM, WHOLE] + [HBM] * 6,
-        out_specs=(WHOLE,) * 6,
+        out_specs=(HBM,) + (WHOLE,) * 5,
         out_shape=(
             shape((length, width), bf16),
             shape((groups,) + qkv[1:], bf16),
@@ -1781,6 +1791,7 @@
             pltpu.VMEM(w_qkv.shape, bf16),
             pltpu.VMEM((length, width), bf16),
             pltpu.VMEM((width, length), bf16),
+            pltpu.VMEM((length, width), bf16),
             pltpu.VMEM((length, width), bf16),
         ]
         + buffers

time: 217 us -> 216 us (level)
  no operation moved by 1% of the time
where the time goes in v1:
time: 216 us
  Pallas kernels  213 us (99%)
    pallas_call x1, Pallas kernels, run_sum_backward(): pl.pallas_call(partial(sum_backward_kernel, shards), in_specs=[HBM, WHOLE...  74.1 us
    pallas_call x1, Pallas kernels, run_sum_hidden(): pl.pallas_call(partial(sum_hidden_kernel, shards), in_specs=[HBM] * 3 + [...  71.2 us
    pallas_call x1, Pallas kernels, run_gather_forward(): pl.pallas_call(partial(gather_forward_kernel, shards), in_specs=[WHOLE] *...  61.9 us
    pallas_call x1, Pallas kernels, run_finish(): pl.pallas_call(partial(finish_kernel, shards), in_specs=[WHOLE] * 9, out_...  5.97 us

profile of v1, /device:TPU:0, one launch (start us, length us, event | category | flops | bytes accessed | tf_op | source)
XLA Modules:
  0.0 216.0 jit_solution(12018960483979224125)
XLA Ops:
  0.6 0.8 stack.35
  1.4 1.3 fusion.2.own_params_ref
  2.7 61.9 %gather_forward.1 = (bf16[3,1024,768]{2,1,0:T(8,128)(2,1)}, bf16[768,1024]{1,0:T(8,128)(2,1)}, f32[16,1024]{1,0:T(8,128)}, f32[16,1024]{1,0:T(8,128)}, bf16[3,8,...) custom-call(bf16[1024,768]{1,0:T(8,128)(2,1)} %tokens_in_ref.3, ...), custom_call_target="tpu_custom_call" | custom-call | tf_op jit(solution)/shard_map/gather_forward/pallas_call | solution.py:1632
  64.6 71.2 %sum_hidden.1 = (bf16[1024,768]{1,0:T(8,128)(2,1)}, f32[1024,768]{1,0:T(8,128)}, bf16[1024,768]{1,0:T(8,128)(2,1)}, bf16[8,96,768]{2,1,0:T(8,128)(2,1)}, bf16[2,...) custom-call(bf16[768,1024]{1,0:T(8,128)(2,1)} %get-tuple-element.54., ...), custom_call_target="tpu_custom_call" | custom-call | tf_op jit(solution)/shard_map/sum_hidden/pallas_call | solution.py:1687
  135.7 74.1 %sum_backward.1 = (bf16[1024,768]{1,0:T(8,128)(2,1)}, bf16[3,96,768]{2,1,0:T(8,128)(2,1)}, bf16[96,768]{1,0:T(8,128)(2,1)}, bf16[2,96,1024]{2,1,0:T(8,128)(2,1)}...) custom-call(bf16[1024,768]{1,0:T(8,128)(2,1)} %tokens_in_ref.3, s32[1,1024]{1,0:T(1,128)} %segment_ref.3, ...), custom_call_target="tpu_custom_call" | custom-call | tf_op jit(solution)/shard_map/sum_backward/pallas_call | solution.py:1765
  209.8 6.0 %finish.1 = (f32[96,2304]{1,0:T(8,128)}, f32[96,768]{1,0:T(8,128)}, f32[96,3072]{1,0:T(8,128)}, f32[384,768]{1,0:T(8,128)}, bf16[1024,768]{1,0:T(8,128)(2,1)}, /...) custom-call(bf16[3,96,768]{2,1,0:T(8,128)(2,1)} %get-tuple-element.6, ...), custom_call_target="tpu_custom_call" | custom-call | tf_op jit(solution)/shard_map/finish/pallas_call | solution.py:1828
